TPU v7x, 32 devices: a whole 2x2x4 slice. The times are simulated.
32 devices in a mesh: dp: 8 (over y, x, core), tensor: 4 (over z).
Axes of the slice: x: 2, y: 2, z: 4, core: 2. Of those that a mesh axis runs over, the one named last changes fastest.
Arguments:
- wq_flat: bfloat16 [8192, 4096], P(('dp', 'tensor')), may hold values from -0.125 to 0.125
- hidden: bfloat16 [4, 16, 8192], P(None, 'dp'), may hold values from -6 to 6
- cache: bfloat16 [16, 4, 8192, 256], P('dp', None, 'tensor'), may hold values from -300 to 300
- new_kv: bfloat16 [4, 16, 4, 256], P(None, 'dp'), may hold values from -6 to 6
- lengths: int32 [16], P('dp'), may hold values from 1 to 8192, as said below
Outputs:
- attended: bfloat16 [4, 16, 4096], P(None, 'dp', 'tensor')
Inputs may be any that keep to these rules, and one draw needn't show every extreme that they name: `lengths`: every sequence has at least one cached position; in every draw some sequence has exactly 8192.
All inputs are finite; a program needn't handle non-finite values.
Results may differ from a plain program's by a relative error of at most 0.03.
Values may be sent and summed in bfloat16 or wider, within the bound.
A program may use at most 64 MiB of HBM per device.

v0:
```python
import functools

import jax
import jax.numpy as jnp
from jax import lax
from jax.experimental import pallas as pl
from jax.experimental.pallas import tpu as pltpu
from jax.sharding import PartitionSpec as P

QH = 32
HD = 128
MESH = pl.DeviceIdType.MESH
NEG = -1e30


def kernel(
    n,
    nt,
    blocked,
    lengths,
    hid_any,
    blocks,
    new_any,
    wq,
    cache,
    out,
    hid,
    new_kv,
    sem_in,
    wq_own,
    wq_other,
    kv,
    fresh,
    x_sc,
    xg,
    yown,
    ysend,
    yrecv,
    psend,
    precv,
    zsend,
    zrecv,
    qsend,
    qbuf,
    q_sc,
    acc_sc,
    asend,
    arecv,
    m_sc,
    l_sc,
    ssend,
    srecv,
    sem_w,
    sem_kv,
    sx_s,
    sx_r,
    sy_s,
    sy_r,
    sp_s,
    sp_r,
    sz_s,
    sz_r,
    sq_s,
    sq_r,
    sa_s,
    sa_r,
    ss_s,
    ss_r,
):
    d = lax.axis_index("dp")
    t = lax.axis_index("tensor")
    core = lax.rem(d, 2)
    chip = d // 2
    chips = n // 2
    mate = d + 1 - 2 * core
    steps, seqs, width = hid.shape
    depth = wq_own.shape[0]
    rows = steps * seqs
    half = wq_own.shape[1]
    _, kvh, ctx, _ = kv.shape
    drains = []
    heads = QH // nt
    group = QH // kvh
    scale = 1.0 / HD**0.5

    load_hid = pltpu.make_async_copy(hid_any, hid, sem_in.at[0])
    load_new = pltpu.make_async_copy(new_any, new_kv, sem_in.at[1])
    load_hid.start()
    load_new.start()
    load_other = pltpu.make_async_copy(
        wq.at[:, pl.ds(pl.multiple_of((1 - core) * half, half), half)], wq_other, sem_w.at[0]
    )
    load_own = pltpu.make_async_copy(
        wq.at[:, pl.ds(pl.multiple_of(core * half, half), half)], wq_own, sem_w.at[1]
    )
    load_other.start()
    load_own.start()
    load_kv = [
        [pltpu.make_async_copy(cache.at[s, g], kv.at[s, g], sem_kv.at[s, g]) for g in range(kvh)]
        for s in range(seqs)
    ]
    for g in range(kvh):
        for s in range(seqs):
            load_kv[s][g].start()

    barrier = pltpu.get_barrier_semaphore()

    @pl.loop(1, n)
    def _(k):
        pl.semaphore_signal(
            barrier, inc=1, device_id=(lax.rem(d + k, n), t), device_id_type=MESH
        )

    @pl.loop(1, nt)
    def _(k):
        peer = lax.rem(t + k, nt)
        pl.semaphore_signal(barrier, inc=1, device_id=(d, peer), device_id_type=MESH)
        pl.semaphore_signal(barrier, inc=1, device_id=(mate, peer), device_id_type=MESH)

    pl.semaphore_wait(barrier, n - 1 + 2 * (nt - 1))

    load_hid.wait()
    load_new.wait()

    def columns_of(peer):
        if blocked:
            return blocks.at[peer]
        start = pl.multiple_of((peer * nt + t) * depth, depth)
        return hid.at[:, :, pl.ds(start, depth)]

    def x_copy(k, slot, peer, source):
        return pltpu.make_async_remote_copy(
            src_ref=columns_of(peer),
            dst_ref=xg.at[slot],
            send_sem=sx_s.at[k],
            recv_sem=sx_r.at[source],
            device_id=(peer, t),
            device_id_type=MESH,
        )

    @pl.loop(1, n)
    def _(k):
        x_copy(k, d, lax.rem(d + k, n), d).start()

    xg[d] = columns_of(d)[...]
    for i in range(steps):
        for s in range(seqs):
            r = (i * seqs + s) * kvh
            fresh[r : r + kvh, :] = new_kv[i, s].astype(jnp.float32)
    load_other.wait()
    load_own.wait()

    @pl.loop(1, n)
    def _(k):
        peer = lax.rem(d + k, n)
        x_copy(k, peer, peer, peer).wait_recv()

    drains.append(lambda: pl.loop(1, n)(lambda k: x_copy(k, d, lax.rem(d + k, n), d).wait_send()))
    if blocked:
        x = xg[...].reshape(n * rows, depth).astype(jnp.bfloat16)
    else:
        for p in range(n):
            for i in range(steps):
                r = p * rows + i * seqs
                x_sc[r : r + seqs, :] = xg[p, i].astype(jnp.float32)
        x = x_sc[...].astype(jnp.bfloat16)

    cuts = psend.shape[0]
    wide = half // cuts

    def p_copy(c, p):
        return pltpu.make_async_remote_copy(
            src_ref=psend.at[c, p],
            dst_ref=precv.at[c, p],
            send_sem=sp_s.at[c, p],
            recv_sem=sp_r.at[c, p],
            device_id=(mate, t),
            device_id_type=MESH,
        )

    def order(k):
        return lax.rem(chip + chips - k, chips)

    for c in range(cuts):
        psend[c] = (
            jnp.dot(
                x, wq_other[:, c * wide : (c + 1) * wide], preferred_element_type=jnp.float32
            )
            .astype(jnp.bfloat16)
            .reshape(chips, 2 * rows, wide)
        )

        @pl.loop(1, chips + 1)
        def _(k):
            p_copy(c, order(k)).start()

    for c in range(cuts):
        yown[c] = jnp.dot(
            x, wq_own[:, c * wide : (c + 1) * wide], preferred_element_type=jnp.float32
        ).reshape(chips, 2 * rows, wide)

    def p_drain():
        for c in range(cuts):
            pl.loop(1, chips + 1)(lambda k: p_copy(c, order(k)).wait_send())

    drains.append(p_drain)

    def y_copy(c, k, slot, peer, source):
        return pltpu.make_async_remote_copy(
            src_ref=ysend.at[c, peer],
            dst_ref=yrecv.at[c, slot],
            send_sem=sy_s.at[c, k],
            recv_sem=sy_r.at[c, source],
            device_id=(2 * peer + core, t),
            device_id_type=MESH,
        )

    for c in range(cuts):

        @pl.loop(1, chips)
        def _(k):
            p = order(k)
            p_copy(c, p).wait_recv()
            ysend[c, p] = (yown[c, p] + precv[c, p].astype(jnp.float32)).astype(jnp.bfloat16)
            y_copy(c, k, chip, p, chip).start()

        p_copy(c, chip).wait_recv()

    part = wide // nt

    def z_copy(c, k, slot, peer, source):
        return pltpu.make_async_remote_copy(
            src_ref=zsend.at[c, peer],
            dst_ref=zrecv.at[c, slot],
            send_sem=sz_s.at[c, k],
            recv_sem=sz_r.at[c, source],
            device_id=(d, peer),
            device_id_type=MESH,
        )

    for c in range(cuts):

        def y_add(k, z):
            p = order(k)
            y_copy(c, k, p, p, p).wait_recv()
            return z + yrecv[c, p].astype(jnp.float32)

        z = lax.fori_loop(1, chips, y_add, yown[c, chip] + precv[c, chip].astype(jnp.float32))
        for j in range(nt):
            zsend[c, j] = z[:, j * part : (j + 1) * part].astype(zsend.dtype)

        @pl.loop(1, nt)
        def _(k):
            z_copy(c, k, t, lax.rem(t + k, nt), t).start()

    def yz_drain():
        for c in range(cuts):
            pl.loop(1, chips)(lambda k: y_copy(c, k, chip, order(k), chip).wait_send())
            pl.loop(1, nt)(lambda k: z_copy(c, k, t, lax.rem(t + k, nt), t).wait_send())

    drains.append(yz_drain)

    def q_copy(c, k, which, peer_core, peer, slot):
        return pltpu.make_async_remote_copy(
            src_ref=qsend.at[c, peer_core],
            dst_ref=qbuf.at[c, slot],
            send_sem=sq_s.at[c, k, which],
            recv_sem=sq_r.at[c, slot],
            device_id=(2 * chip + peer_core, peer),
            device_id_type=MESH,
        )

    mine = core * nt + t
    for c in range(cuts):

        def z_add(k, total):
            peer = lax.rem(t + k, nt)
            z_copy(c, k, peer, peer, peer).wait_recv()
            return total + zrecv[c, peer].astype(jnp.float32)

        piece = lax.fori_loop(1, nt, z_add, zsend[c, t].astype(jnp.float32))
        for i in range(2):
            qsend[c, i] = piece[i * rows : (i + 1) * rows].astype(jnp.bfloat16)

        @pl.loop(1, nt)
        def _(k):
            peer = lax.rem(t + k, nt)
            q_copy(c, k, 0, core, peer, mine).start()
            q_copy(c, k, 1, 1 - core, peer, mine).start()

        q_copy(c, 0, 1, 1 - core, t, mine).start()
        qbuf[c, mine] = qsend[c, core]

    def q_drain():
        for c in range(cuts):
            q_copy(c, 0, 1, 1 - core, t, mine).wait_send()

            @pl.loop(1, nt)
            def _(k):
                peer = lax.rem(t + k, nt)
                q_copy(c, k, 0, core, peer, mine).wait_send()
                q_copy(c, k, 1, 1 - core, peer, mine).wait_send()

    drains.append(q_drain)

    band = group * rows
    position = t * ctx + lax.broadcasted_iota(jnp.int32, (1, ctx), 1)
    owned = heads * rows
    eye = lax.broadcasted_iota(jnp.int32, (owned, HD), 0) == lax.broadcasted_iota(
        jnp.int32, (owned, HD), 1
    )

    def a_copy(slot, peer, source):
        return pltpu.make_async_remote_copy(
            src_ref=asend.at[peer],
            dst_ref=arecv.at[slot],
            send_sem=sa_s.at[peer],
            recv_sem=sa_r.at[source],
            device_id=(d, peer),
            device_id_type=MESH,
        )

    def s_copy(slot, peer, source):
        return pltpu.make_async_remote_copy(
            src_ref=ssend.at[peer],
            dst_ref=srecv.at[slot],
            send_sem=ss_s.at[peer],
            recv_sem=ss_r.at[source],
            device_id=(d, peer),
            device_id_type=MESH,
        )

    def attend(g, s):
        base = pl.ds(pl.multiple_of(g * band, band), band)
        span = pl.ds(s, group * steps, stride=seqs)
        q = q_sc.at[base][span, :].astype(jnp.bfloat16)
        scores = lax.dot_general(
            q, kv[s, g, :, :HD], (((1,), (1,)), ((), ())), preferred_element_type=jnp.float32
        )
        masked = jnp.where(position < lengths[s], scores * scale, NEG)
        best = jnp.max(masked, axis=-1, keepdims=True)
        weights = jnp.exp(masked - best)
        total = jnp.sum(weights, axis=-1, keepdims=True)
        acc = jnp.dot(
            weights.astype(jnp.bfloat16), kv[s, g, :, HD:], preferred_element_type=jnp.float32
        )
        acc_sc.at[base][span, :] = acc
        m_sc.at[base][span, :] = jnp.broadcast_to(best, acc.shape)
        l_sc.at[base][span, :] = jnp.broadcast_to(total, acc.shape)

    heads_slot = part // HD
    side = kvh // 2 // cuts
    per = group // heads
    far = (2 * t < nt).astype(jnp.int32)
    for c in range(cuts):
        q_copy(c, 0, 1, 1 - core, t, (1 - core) * nt + t).wait_recv()

        @pl.loop(1, nt)
        def _(k):
            peer = lax.rem(t + k, nt)
            q_copy(c, k, 0, core, peer, core * nt + peer).wait_recv()
            q_copy(c, k, 1, core, peer, (1 - core) * nt + peer).wait_recv()

        for slot in range(2 * nt):
            block = qbuf[c, slot].astype(jnp.float32)
            first = (slot // nt * half + c * wide) // HD + slot % nt * heads_slot
            for j in range(heads_slot):
                h = first + j
                q_sc[h * rows : (h + 1) * rows, :] = block[:, j * HD : (j + 1) * HD]

        ready = [i * (kvh // 2) + c * side + j for i in range(2) for j in range(side)]
        for g in ready:
            for s in range(seqs):
                load_kv[s][g].wait()
        for low, high in zip(ready, ready[::-1]):
            g = low + (high - low) * far
            for s in range(seqs):
                attend(g, s)
            for i in range(per):
                j = g * per + i
                window = pl.ds(pl.multiple_of(j * owned, owned), owned)
                asend[j] = acc_sc[window, :].astype(asend.dtype)
                for at, ref in enumerate((m_sc, l_sc)):
                    ssend[j, at : at + 1, :] = jnp.sum(
                        jnp.where(eye, ref[window, :], 0.0), axis=0, keepdims=True
                    )

                @pl.when(t != j)
                def _():
                    a_copy(t, j, t).start()
                    s_copy(t, j, t).start()

    own = pl.ds(pl.multiple_of(t * owned, owned), owned)
    q_own = q_sc[own, :].astype(jnp.bfloat16)
    new_keys = fresh[:, :HD].astype(jnp.bfloat16)
    new_values = fresh[:, HD:].astype(jnp.bfloat16)
    new_scores = (
        lax.dot_general(
            q_own, new_keys, (((1,), (1,)), ((), ())), preferred_element_type=jnp.float32
        )
        * scale
    )
    row = lax.broadcasted_iota(jnp.int32, new_scores.shape, 0)
    col = lax.broadcasted_iota(jnp.int32, new_scores.shape, 1)
    col_row = col // kvh
    causal = (
        (lax.rem(col, kvh) == t * heads // group)
        & (lax.rem(row, seqs) == lax.rem(col_row, seqs))
        & (lax.rem(row, rows) // seqs >= col_row // seqs)
    )
    new_masked = jnp.where(causal, new_scores, NEG)
    top = jnp.max(new_masked, axis=-1, keepdims=True)
    new_weights = jnp.where(causal, jnp.exp(new_masked - top), 0.0)
    denom = jnp.sum(new_weights, axis=-1, keepdims=True)
    accum = jnp.dot(
        new_weights.astype(jnp.bfloat16), new_values, preferred_element_type=jnp.float32
    )

    def join(state, best, total, acc):
        top, denom, accum = state
        peak = jnp.maximum(top, best)
        left = jnp.exp(top - peak)
        right = jnp.exp(best - peak)
        return peak, denom * left + total * right, accum * left + acc * right

    state = join((top, denom, accum), m_sc[own, :][:, :1], l_sc[own, :][:, :1], acc_sc[own, :])

    def a_join(k, state):
        peer = lax.rem(t + k, nt)
        a_copy(peer, peer, peer).wait_recv()
        s_copy(peer, peer, peer).wait_recv()
        stats = srecv[peer]
        best = jnp.sum(jnp.where(eye, stats[0:1, :], 0.0), axis=1, keepdims=True)
        total = jnp.sum(jnp.where(eye, stats[1:2, :], 0.0), axis=1, keepdims=True)
        return join(state, best, total, arecv[peer].astype(jnp.float32))

    top, denom, accum = lax.fori_loop(1, nt, a_join, state)
    result = accum / denom
    for j in range(heads):
        for i in range(steps):
            r = j * rows + i * seqs
            out[i, :, j * HD : (j + 1) * HD] = result[r : r + seqs].astype(out.dtype)

    def a_drain():
        @pl.loop(1, nt)
        def _(k):
            peer = lax.rem(t + k, nt)
            a_copy(t, peer, t).wait_send()
            s_copy(t, peer, t).wait_send()

    drains.append(a_drain)
    for drain in drains:
        drain()


def body(wq_flat, hidden, cache, new_kv, lengths):
    nt = lax.axis_size("tensor")
    n = lax.axis_size("dp")
    t = lax.axis_index("tensor")
    steps, seqs, width = hidden.shape
    rows = steps * seqs
    depth, columns = wq_flat.shape
    kvh, ctx = cache.shape[1], cache.shape[2]
    half = columns // 2
    cuts = 2 if half // (2 * nt) % HD == 0 and kvh % 4 == 0 else 1
    wide = half // cuts
    part = wide // nt
    heads = QH // nt
    owned = heads * rows
    chips = n // 2
    bf16, f32 = jnp.bfloat16, jnp.float32
    dma = pltpu.SemaphoreType.DMA
    vmem = pl.BlockSpec(memory_space=pltpu.VMEM)
    blocked = depth % 128 != 0
    blocks = hidden
    if blocked:
        blocks = hidden.reshape(rows, n, nt, depth)
        blocks = lax.dynamic_index_in_dim(blocks, t, 2, keepdims=False).astype(f32)
        blocks = blocks.transpose(1, 0, 2)
    held = (rows, depth) if blocked else (steps, seqs, depth)
    anywhere = pl.BlockSpec(memory_space=pl.ANY)
    result = pl.pallas_call(
        functools.partial(kernel, n, nt, blocked),
        out_shape=pltpu.VMEM((steps, seqs, heads * HD), f32),
        in_specs=[pl.BlockSpec(memory_space=pltpu.SMEM), anywhere, vmem if blocked else anywhere, anywhere, anywhere, anywhere],
        out_specs=vmem,
        scratch_shapes=[
            pltpu.VMEM(hidden.shape, bf16),
            pltpu.VMEM(new_kv.shape, bf16),
            dma((2,)),
            pltpu.VMEM((depth, half), bf16),
            pltpu.VMEM((depth, half), bf16),
            pltpu.VMEM(cache.shape, bf16),
            pltpu.VMEM((rows * kvh, 2 * HD), f32),
            pltpu.VMEM((n * rows, depth), f32),
            pltpu.VMEM((n, *held), blocks.dtype),
            pltpu.VMEM((cuts, chips, 2 * rows, wide), f32),
            pltpu.VMEM((cuts, chips, 2 * rows, wide), bf16),
            pltpu.VMEM((cuts, chips, 2 * rows, wide), bf16),
            pltpu.VMEM((cuts, chips, 2 * rows, wide), bf16),
            pltpu.VMEM((cuts, chips, 2 * rows, wide), bf16),
            pltpu.VMEM((cuts, nt, 2 * rows, part), bf16),
            pltpu.VMEM((cuts, nt, 2 * rows, part), bf16),
            pltpu.VMEM((cuts, 2, rows, part), bf16),
            pltpu.VMEM((cuts, 2 * nt, rows, part), bf16),
            pltpu.VMEM((QH * rows, HD), f32),
            pltpu.VMEM((QH * rows, HD), f32),
            pltpu.VMEM((nt, owned, HD), bf16),
            pltpu.VMEM((nt, owned, HD), bf16),
            pltpu.VMEM((QH * rows, HD), f32),
            pltpu.VMEM((QH * rows, HD), f32),
            pltpu.VMEM((nt, 8, HD), f32),
            pltpu.VMEM((nt, 8, HD), f32),
            dma((2,)),
            dma((seqs, kvh)),
            dma((n,)),
            dma((n,)),
            dma((cuts, chips)),
            dma((cuts, chips)),
            dma((cuts, chips)),
            dma((cuts, chips)),
            dma((cuts, nt)),
            dma((cuts, nt)),
            dma((cuts, nt, 2)),
            dma((cuts, 2 * nt)),
            dma((nt,)),
            dma((nt,)),
            dma((nt,)),
            dma((nt,)),
        ],
        compiler_params=pltpu.CompilerParams(collective_id=0, has_side_effects=True),
    )(lengths, hidden, blocks, new_kv, wq_flat, cache)
    return result.astype(bf16)


def solution(mesh):
    placed = (
        P(("dp", "tensor"), None),
        P(None, "dp", None),
        P("dp", None, "tensor", None),
        P(None, "dp", None, None),
        P("dp"),
    )
    return jax.shard_map(
        body, mesh=mesh, in_specs=placed, out_specs=P(None, "dp", "tensor"), check_vma=False
    )
```

profile of v0, /device:TPU:0, one launch (start us, length us, event | category | flops | bytes accessed | tf_op | source)
XLA Modules:
  0.0 29.9 jit_solution(11105400480523567952)
XLA Ops:
  0.0 29.3 %shard_map.55 = f32[4,2,1024]{2,1,0:T(2,128)S(1)} custom-call(s32[2]{0:T(128)} %lengths.1, bf16[4,2,8192]{2,1,0:T(2,128)(2,1)} %blocks.1, bf16[4,2,8192]{2,1,0:T(2,128)(2,1)} %blocks.1, bf16[4,2,4,256]{3,2,1,0:T(4,128)(2,1)} %new_any.1, bf16[256,4096]{1,0:T(8,128)(2,1)} %wq.1, bf16[2,4,2048,256]{3,2,1,0:T(8,128)(2,1)} %cache.1), custom_call_target="tpu_custom_call" | custom-call | tf_op jit(solution)/shard_map/pallas_call | solution.py:482
  29.3 0.6 %convert_element_type.3 = bf16[4,2,1024]{2,1,0:T(2,128)(2,1)} convert(f32[4,2,1024]{2,1,0:T(2,128)S(1)} %shard_map.55) | non-fusion elementwise | flops 8192 | bytes 49152 | tf_op jit(solution)/shard_map/convert_element_type | solution.py:533
where the time goes:
time: 30.1 us; the launch traced here: 29.9 us
  Pallas kernels  29.3 us (97%)
  other arithmetic  0.62 us (2%)
    pallas_call x1, Pallas kernels, body(): pl.pallas_call(functools.partial(kernel, n, nt, blocked), out_shape=pltpu...  29.3 us
    convert_element_type x1, other arithmetic, body(): return result.astype(bf16)  0.62 us

commit v1 on v0

--- a/solution.py
+++ b/solution.py
@@ -27,8 +27,8 @@
     hid,
     new_kv,
     sem_in,
-    wq_own,
-    wq_other,
+    wq_out,
+    wq_all,
     kv,
     fresh,
     x_sc,
@@ -36,11 +36,7 @@
     yown,
     ysend,
     yrecv,
-    psend,
-    precv,
     zsend,
-    zrecv,
-    qsend,
     qbuf,
     q_sc,
     acc_sc,
@@ -58,8 +54,6 @@
     sy_r,
     sp_s,
     sp_r,
-    sz_s,
-    sz_r,
     sq_s,
     sq_r,
     sa_s,
@@ -74,9 +68,8 @@
     chips = n // 2
     mate = d + 1 - 2 * core
     steps, seqs, width = hid.shape
-    depth = wq_own.shape[0]
+    _, depth, half = wq_all.shape
     rows = steps * seqs
-    half = wq_own.shape[1]
     _, kvh, ctx, _ = kv.shape
     drains = []
     heads = QH // nt
@@ -87,22 +80,18 @@
     load_new = pltpu.make_async_copy(new_any, new_kv, sem_in.at[1])
     load_hid.start()
     load_new.start()
-    load_other = pltpu.make_async_copy(
-        wq.at[:, pl.ds(pl.multiple_of((1 - core) * half, half), half)], wq_other, sem_w.at[0]
+    load_out = pltpu.make_async_copy(
+        wq.at[:, pl.ds(pl.multiple_of((1 - core) * half, half), half)], wq_out, sem_w.at[0]
     )
     load_own = pltpu.make_async_copy(
-        wq.at[:, pl.ds(pl.multiple_of(core * half, half), half)], wq_own, sem_w.at[1]
-    )
-    load_other.start()
+        wq.at[:, pl.ds(pl.multiple_of(core * half, half), half)], wq_all.at[core], sem_w.at[1]
+    )
+    load_out.start()
     load_own.start()
     load_kv = [
         [pltpu.make_async_copy(cache.at[s, g], kv.at[s, g], sem_kv.at[s, g]) for g in range(kvh)]
         for s in range(seqs)
     ]
-    for g in range(kvh):
-        for s in range(seqs):
-            load_kv[s][g].start()
-
     barrier = pltpu.get_barrier_semaphore()
 
     @pl.loop(1, n)
@@ -122,88 +111,92 @@
     load_hid.wait()
     load_new.wait()
 
-    def columns_of(peer):
+    def columns_of(block):
         if blocked:
-            return blocks.at[peer]
-        start = pl.multiple_of((peer * nt + t) * depth, depth)
+            return blocks.at[block]
+        start = pl.multiple_of((block * nt + t) * depth, depth)
         return hid.at[:, :, pl.ds(start, depth)]
 
-    def x_copy(k, slot, peer, source):
+    def chip_at(k):
+        return lax.rem(chip % 2 + k % 2, 2) + 2 * lax.rem(chip // 2 + k // 2, chips // 2)
+
+    def peer_at(k):
+        return 2 * chip_at(k // 2) + lax.rem(core + k % 2, 2)
+
+    def x_copy(k, b, slot, peer, source):
         return pltpu.make_async_remote_copy(
-            src_ref=columns_of(peer),
-            dst_ref=xg.at[slot],
-            send_sem=sx_s.at[k],
-            recv_sem=sx_r.at[source],
+            src_ref=columns_of(2 * (peer // 2) + b),
+            dst_ref=xg.at[b, slot],
+            send_sem=sx_s.at[k, b],
+            recv_sem=sx_r.at[source, b],
             device_id=(peer, t),
             device_id_type=MESH,
         )
 
+    push = pltpu.make_async_remote_copy(
+        src_ref=wq_out,
+        dst_ref=wq_all.at[core],
+        send_sem=sp_s.at[core],
+        recv_sem=sp_r.at[core],
+        device_id=(mate, t),
+        device_id_type=MESH,
+    )
+    pull = pltpu.make_async_remote_copy(
+        src_ref=wq_out,
+        dst_ref=wq_all.at[1 - core],
+        send_sem=sp_s.at[core],
+        recv_sem=sp_r.at[1 - core],
+        device_id=(mate, t),
+        device_id_type=MESH,
+    )
+
     @pl.loop(1, n)
     def _(k):
-        x_copy(k, d, lax.rem(d + k, n), d).start()
-
-    xg[d] = columns_of(d)[...]
+        for b in range(2):
+            x_copy(n - k, b, d, peer_at(n - k), d).start()
+
+    load_out.wait()
+    push.start()
+    for b in range(2):
+        xg[b, d] = columns_of(2 * chip + b)[...]
+    for g in range(kvh):
+        for s in range(seqs):
+            load_kv[s][g].start()
     for i in range(steps):
         for s in range(seqs):
             r = (i * seqs + s) * kvh
             fresh[r : r + kvh, :] = new_kv[i, s].astype(jnp.float32)
-    load_other.wait()
     load_own.wait()
+    pull.wait_recv()
 
     @pl.loop(1, n)
     def _(k):
-        peer = lax.rem(d + k, n)
-        x_copy(k, peer, peer, peer).wait_recv()
-
-    drains.append(lambda: pl.loop(1, n)(lambda k: x_copy(k, d, lax.rem(d + k, n), d).wait_send()))
-    if blocked:
-        x = xg[...].reshape(n * rows, depth).astype(jnp.bfloat16)
-    else:
-        for p in range(n):
-            for i in range(steps):
-                r = p * rows + i * seqs
-                x_sc[r : r + seqs, :] = xg[p, i].astype(jnp.float32)
-        x = x_sc[...].astype(jnp.bfloat16)
-
-    cuts = psend.shape[0]
+        peer = peer_at(k)
+        for b in range(2):
+            x_copy(k, b, peer, peer, peer).wait_recv()
+
+    def x_drain():
+        push.wait_send()
+
+        @pl.loop(1, n)
+        def _(k):
+            for b in range(2):
+                x_copy(k, b, d, peer_at(k), d).wait_send()
+
+    drains.append(x_drain)
+    xs = []
+    for b in range(2):
+        if blocked:
+            xs.append(xg[b].reshape(n * rows, depth).astype(jnp.bfloat16))
+        else:
+            for p in range(n):
+                for i in range(steps):
+                    r = p * rows + i * seqs
+                    x_sc[b, r : r + seqs, :] = xg[b, p, i].astype(jnp.float32)
+            xs.append(x_sc[b].astype(jnp.bfloat16))
+
+    cuts = ysend.shape[0]
     wide = half // cuts
-
-    def p_copy(c, p):
-        return pltpu.make_async_remote_copy(
-            src_ref=psend.at[c, p],
-            dst_ref=precv.at[c, p],
-            send_sem=sp_s.at[c, p],
-            recv_sem=sp_r.at[c, p],
-            device_id=(mate, t),
-            device_id_type=MESH,
-        )
-
-    def order(k):
-        return lax.rem(chip + chips - k, chips)
-
-    for c in range(cuts):
-        psend[c] = (
-            jnp.dot(
-                x, wq_other[:, c * wide : (c + 1) * wide], preferred_element_type=jnp.float32
-            )
-            .astype(jnp.bfloat16)
-            .reshape(chips, 2 * rows, wide)
-        )
-
-        @pl.loop(1, chips + 1)
-        def _(k):
-            p_copy(c, order(k)).start()
-
-    for c in range(cuts):
-        yown[c] = jnp.dot(
-            x, wq_own[:, c * wide : (c + 1) * wide], preferred_element_type=jnp.float32
-        ).reshape(chips, 2 * rows, wide)
-
-    def p_drain():
-        for c in range(cuts):
-            pl.loop(1, chips + 1)(lambda k: p_copy(c, order(k)).wait_send())
-
-    drains.append(p_drain)
 
     def y_copy(c, k, slot, peer, source):
         return pltpu.make_async_remote_copy(
@@ -216,53 +209,24 @@
         )
 
     for c in range(cuts):
+        y = sum(
+            jnp.dot(
+                xs[b], wq_all[b, :, c * wide : (c + 1) * wide], preferred_element_type=jnp.float32
+            )
+            for b in range(2)
+        ).reshape(chips, 2 * rows, wide)
+        ysend[c] = y.astype(jnp.bfloat16)
+        yown[c] = y
 
         @pl.loop(1, chips)
         def _(k):
-            p = order(k)
-            p_copy(c, p).wait_recv()
-            ysend[c, p] = (yown[c, p] + precv[c, p].astype(jnp.float32)).astype(jnp.bfloat16)
-            y_copy(c, k, chip, p, chip).start()
-
-        p_copy(c, chip).wait_recv()
-
-    part = wide // nt
-
-    def z_copy(c, k, slot, peer, source):
-        return pltpu.make_async_remote_copy(
-            src_ref=zsend.at[c, peer],
-            dst_ref=zrecv.at[c, slot],
-            send_sem=sz_s.at[c, k],
-            recv_sem=sz_r.at[c, source],
-            device_id=(d, peer),
-            device_id_type=MESH,
-        )
-
-    for c in range(cuts):
-
-        def y_add(k, z):
-            p = order(k)
-            y_copy(c, k, p, p, p).wait_recv()
-            return z + yrecv[c, p].astype(jnp.float32)
-
-        z = lax.fori_loop(1, chips, y_add, yown[c, chip] + precv[c, chip].astype(jnp.float32))
-        for j in range(nt):
-            zsend[c, j] = z[:, j * part : (j + 1) * part].astype(zsend.dtype)
-
-        @pl.loop(1, nt)
-        def _(k):
-            z_copy(c, k, t, lax.rem(t + k, nt), t).start()
-
-    def yz_drain():
-        for c in range(cuts):
-            pl.loop(1, chips)(lambda k: y_copy(c, k, chip, order(k), chip).wait_send())
-            pl.loop(1, nt)(lambda k: z_copy(c, k, t, lax.rem(t + k, nt), t).wait_send())
-
-    drains.append(yz_drain)
+            y_copy(c, chips - k, chip, chip_at(chips - k), chip).start()
+
+    mine = core * nt + t
 
     def q_copy(c, k, which, peer_core, peer, slot):
         return pltpu.make_async_remote_copy(
-            src_ref=qsend.at[c, peer_core],
+            src_ref=zsend.at[c, peer_core],
             dst_ref=qbuf.at[c, slot],
             send_sem=sq_s.at[c, k, which],
             recv_sem=sq_r.at[c, slot],
@@ -270,17 +234,16 @@
             device_id_type=MESH,
         )
 
-    mine = core * nt + t
     for c in range(cuts):
 
-        def z_add(k, total):
-            peer = lax.rem(t + k, nt)
-            z_copy(c, k, peer, peer, peer).wait_recv()
-            return total + zrecv[c, peer].astype(jnp.float32)
-
-        piece = lax.fori_loop(1, nt, z_add, zsend[c, t].astype(jnp.float32))
+        def y_add(k, z):
+            p = chip_at(k)
+            y_copy(c, k, p, p, p).wait_recv()
+            return z + yrecv[c, p].astype(jnp.float32)
+
+        z = lax.fori_loop(1, chips, y_add, yown[c, chip])
         for i in range(2):
-            qsend[c, i] = piece[i * rows : (i + 1) * rows].astype(jnp.bfloat16)
+            zsend[c, i] = z[i * rows : (i + 1) * rows].astype(zsend.dtype)
 
         @pl.loop(1, nt)
         def _(k):
@@ -289,10 +252,11 @@
             q_copy(c, k, 1, 1 - core, peer, mine).start()
 
         q_copy(c, 0, 1, 1 - core, t, mine).start()
-        qbuf[c, mine] = qsend[c, core]
+        qbuf[c, mine] = zsend[c, core]
 
     def q_drain():
         for c in range(cuts):
+            pl.loop(1, chips)(lambda k: y_copy(c, k, chip, chip_at(k), chip).wait_send())
             q_copy(c, 0, 1, 1 - core, t, mine).wait_send()
 
             @pl.loop(1, nt)
@@ -348,7 +312,6 @@
         m_sc.at[base][span, :] = jnp.broadcast_to(best, acc.shape)
         l_sc.at[base][span, :] = jnp.broadcast_to(total, acc.shape)
 
-    heads_slot = part // HD
     side = kvh // 2 // cuts
     per = group // heads
     far = (2 * t < nt).astype(jnp.int32)
@@ -361,12 +324,14 @@
             q_copy(c, k, 0, core, peer, core * nt + peer).wait_recv()
             q_copy(c, k, 1, core, peer, (1 - core) * nt + peer).wait_recv()
 
-        for slot in range(2 * nt):
-            block = qbuf[c, slot].astype(jnp.float32)
-            first = (slot // nt * half + c * wide) // HD + slot % nt * heads_slot
-            for j in range(heads_slot):
+        for i in range(2):
+            total = qbuf[c, i * nt].astype(jnp.float32)
+            for j in range(1, nt):
+                total = total + qbuf[c, i * nt + j].astype(jnp.float32)
+            first = (i * half + c * wide) // HD
+            for j in range(wide // HD):
                 h = first + j
-                q_sc[h * rows : (h + 1) * rows, :] = block[:, j * HD : (j + 1) * HD]
+                q_sc[h * rows : (h + 1) * rows, :] = total[:, j * HD : (j + 1) * HD]
 
         ready = [i * (kvh // 2) + c * side + j for i in range(2) for j in range(side)]
         for g in ready:
@@ -462,9 +427,8 @@
     depth, columns = wq_flat.shape
     kvh, ctx = cache.shape[1], cache.shape[2]
     half = columns // 2
-    cuts = 2 if half // (2 * nt) % HD == 0 and kvh % 4 == 0 else 1
+    cuts = 2 if kvh % 4 == 0 else 1
     wide = half // cuts
-    part = wide // nt
     heads = QH // nt
     owned = heads * rows
     chips = n // 2
@@ -489,20 +453,16 @@
             pltpu.VMEM(new_kv.shape, bf16),
             dma((2,)),
             pltpu.VMEM((depth, half), bf16),
-            pltpu.VMEM((depth, half), bf16),
+            pltpu.VMEM((2, depth, half), bf16),
             pltpu.VMEM(cache.shape, bf16),
             pltpu.VMEM((rows * kvh, 2 * HD), f32),
-            pltpu.VMEM((n * rows, depth), f32),
-            pltpu.VMEM((n, *held), blocks.dtype),
+            pltpu.VMEM((2, n * rows, depth), f32),
+            pltpu.VMEM((2, n, *held), blocks.dtype),
             pltpu.VMEM((cuts, chips, 2 * rows, wide), f32),
             pltpu.VMEM((cuts, chips, 2 * rows, wide), bf16),
             pltpu.VMEM((cuts, chips, 2 * rows, wide), bf16),
-            pltpu.VMEM((cuts, chips, 2 * rows, wide), bf16),
-            pltpu.VMEM((cuts, chips, 2 * rows, wide), bf16),
-            pltpu.VMEM((cuts, nt, 2 * rows, part), bf16),
-            pltpu.VMEM((cuts, nt, 2 * rows, part), bf16),
-            pltpu.VMEM((cuts, 2, rows, part), bf16),
-            pltpu.VMEM((cuts, 2 * nt, rows, part), bf16),
+            pltpu.VMEM((cuts, 2, rows, wide), bf16),
+            pltpu.VMEM((cuts, 2 * nt, rows, wide), bf16),
             pltpu.VMEM((QH * rows, HD), f32),
             pltpu.VMEM((QH * rows, HD), f32),
             pltpu.VMEM((nt, owned, HD), bf16),
@@ -513,14 +473,12 @@
             pltpu.VMEM((nt, 8, HD), f32),
             dma((2,)),
             dma((seqs, kvh)),
-            dma((n,)),
-            dma((n,)),
+            dma((n, 2)),
+            dma((n, 2)),
             dma((cuts, chips)),
             dma((cuts, chips)),
-            dma((cuts, chips)),
-            dma((cuts, chips)),
-            dma((cuts, nt)),
-            dma((cuts, nt)),
+            dma((2,)),
+            dma((2,)),
             dma((cuts, nt, 2)),
             dma((cuts, 2 * nt)),
             dma((nt,)),

time: 30.1 us -> 25.9 us (0.86)
  Pallas kernels: 29.3 us -> 25.1 us
    pallas_call x1, Pallas kernels: 29.3 us -> 25.1 us  [body(): pl.pallas_call(functools.partial(kernel, n, nt, blocked), out_shape=pltpu...]
where the time goes in v1:
time: 25.9 us; the launch traced here: 25.7 us
  Pallas kernels  25.1 us (97%)
  other arithmetic  0.62 us (2%)
    pallas_call x1, Pallas kernels, body(): pl.pallas_call(functools.partial(kernel, n, nt, blocked), out_shape=pltpu...  25.1 us
    convert_element_type x1, other arithmetic, body(): return result.astype(bf16)  0.62 us

profile of v1, /device:TPU:0, one launch (start us, length us, event | category | flops | bytes accessed | tf_op | source)
XLA Modules:
  0.0 25.7 jit_solution(6416246621795765420)
XLA Ops:
  0.0 25.1 %shard_map.55 = f32[4,2,1024]{2,1,0:T(2,128)S(1)} custom-call(s32[2]{0:T(128)} %lengths.1, bf16[4,2,8192]{2,1,0:T(2,128)(2,1)} %blocks.1, bf16[4,2,8192]{2,1,0:T(2,128)(2,1)} %blocks.1, bf16[4,2,4,256]{3,2,1,0:T(4,128)(2,1)} %new_any.1, bf16[256,4096]{1,0:T(8,128)(2,1)} %wq.1, bf16[2,4,2048,256]{3,2,1,0:T(8,128)(2,1)} %cache.1), custom_call_target="tpu_custom_call" | custom-call | tf_op jit(solution)/shard_map/pallas_call | solution.py:446
  25.1 0.6 %convert_element_type.3 = bf16[4,2,1024]{2,1,0:T(2,128)(2,1)} convert(f32[4,2,1024]{2,1,0:T(2,128)S(1)} %shard_map.55) | non-fusion elementwise | flops 8192 | bytes 49152 | tf_op jit(solution)/shard_map/convert_element_type | solution.py:491

commit v2 on v1

v2 whole, which is shorter than its diff:
```python
import functools

import jax
import jax.numpy as jnp
from jax import lax
from jax.experimental import pallas as pl
from jax.experimental.pallas import tpu as pltpu
from jax.sharding import PartitionSpec as P

QH = 32
HD = 128
MESH = pl.DeviceIdType.MESH
NEG = -1e30


def kernel(
    n,
    nt,
    blocked,
    lengths_any,
    hid_any,
    blocks,
    new_any,
    wq,
    cache,
    out,
    hid,
    new_kv,
    lengths,
    sem_in,
    wq_out,
    wq_all,
    kv,
    fresh,
    x_sc,
    xg,
    yown,
    ysend,
    yrecv,
    zsend,
    qbuf,
    q_sc,
    r_sc,
    asend,
    arecv,
    ssend,
    srecv,
    sem_w,
    sem_kv,
    sx_s,
    sx_r,
    sy_s,
    sy_r,
    sp_s,
    sp_r,
    sq_s,
    sq_r,
    sa_s,
    sa_r,
    ss_s,
    ss_r,
):
    d = lax.axis_index("dp")
    t = lax.axis_index("tensor")
    core = lax.rem(d, 2)
    chip = d // 2
    chips = n // 2
    mate = d + 1 - 2 * core
    steps, seqs, width = hid.shape
    _, depth, half = wq_all.shape
    rows = steps * seqs
    _, kvh, ctx, _ = kv.shape
    drains = []
    heads = QH // nt
    group = QH // kvh
    scale = 1.0 / HD**0.5

    load_hid = pltpu.make_async_copy(hid_any, hid, sem_in.at[0])
    load_new = pltpu.make_async_copy(new_any, new_kv, sem_in.at[1])
    load_lengths = pltpu.make_async_copy(lengths_any, lengths, sem_in.at[2])
    load_hid.start()
    load_lengths.start()
    load_new.start()
    load_out = pltpu.make_async_copy(
        wq.at[:, pl.ds(pl.multiple_of((1 - core) * half, half), half)], wq_out, sem_w.at[0]
    )
    load_own = pltpu.make_async_copy(
        wq.at[:, pl.ds(pl.multiple_of(core * half, half), half)], wq_all.at[core], sem_w.at[1]
    )
    load_out.start()
    load_own.start()
    load_kv = [
        [pltpu.make_async_copy(cache.at[s, g], kv.at[s, g], sem_kv) for g in range(kvh)]
        for s in range(seqs)
    ]
    barrier = pltpu.get_barrier_semaphore()

    @pl.loop(1, n)
    def _(k):
        pl.semaphore_signal(
            barrier, inc=1, device_id=(lax.rem(d + k, n), t), device_id_type=MESH
        )

    @pl.loop(1, nt)
    def _(k):
        peer = lax.rem(t + k, nt)
        pl.semaphore_signal(barrier, inc=1, device_id=(d, peer), device_id_type=MESH)
        pl.semaphore_signal(barrier, inc=1, device_id=(mate, peer), device_id_type=MESH)

    pl.semaphore_wait(barrier, n - 1 + 2 * (nt - 1))

    load_hid.wait()
    load_new.wait()
    load_lengths.wait()

    def columns_of(block):
        if blocked:
            return blocks.at[block]
        start = pl.multiple_of((block * nt + t) * depth, depth)
        return hid.at[:, :, pl.ds(start, depth)]

    def whole(ref, send_sem, recv_sem):
        return pltpu.make_async_remote_copy(
            src_ref=ref,
            dst_ref=ref,
            send_sem=send_sem,
            recv_sem=recv_sem,
            device_id=(mate, t),
            device_id_type=MESH,
        )

    def chip_at(k):
        return lax.rem(chip % 2 + k % 2, 2) + 2 * lax.rem(chip // 2 + k // 2, chips // 2)

    def peer_at(k):
        return 2 * chip_at(k // 2) + lax.rem(core + k % 2, 2)

    def x_copy(b, peer):
        return pltpu.make_async_remote_copy(
            src_ref=columns_of(2 * (peer // 2) + b),
            dst_ref=xg.at[b, d],
            send_sem=sx_s,
            recv_sem=sx_r,
            device_id=(peer, t),
            device_id_type=MESH,
        )

    push = pltpu.make_async_remote_copy(
        src_ref=wq_out,
        dst_ref=wq_all.at[core],
        send_sem=sp_s,
        recv_sem=sp_r,
        device_id=(mate, t),
        device_id_type=MESH,
    )
    @pl.loop(1, n)
    def _(k):
        for b in range(2):
            x_copy(b, peer_at(n - k)).start()

    load_out.wait()
    push.start()
    for b in range(2):
        xg[b, d] = columns_of(2 * chip + b)[...]
    for g in range(kvh):
        for s in range(seqs):
            load_kv[s][g].start()
    for i in range(steps):
        for s in range(seqs):
            r = (i * seqs + s) * kvh
            fresh[r : r + kvh, :] = new_kv[i, s].astype(jnp.float32)
    load_own.wait()
    push.wait_recv()

    x_all = whole(xg.at[:, pl.ds(0, n - 1)], sx_s, sx_r)
    x_all.wait_recv()
    drains.append(push.wait_send)
    drains.append(x_all.wait_send)
    _, tiles, _, lanes = x_sc.shape
    xs = []
    for b in range(2):
        for p in range(n):
            if blocked:
                for s in range(seqs):
                    r = (s * n + p) * steps
                    x_sc[b, 0, r : r + steps, :] = xg[b, p, s * steps : (s + 1) * steps]
            else:
                for i in range(steps):
                    lines = pl.ds(p * steps + i, seqs, stride=n * steps)
                    block = xg[b, p, i].astype(jnp.float32)
                    for h in range(tiles):
                        x_sc.at[b, h][lines, :] = block[:, h * lanes : (h + 1) * lanes]
        xs.append(jnp.concatenate([x_sc[b, h] for h in range(tiles)], axis=1).astype(jnp.bfloat16))

    cuts = ysend.shape[0]
    wide = half // cuts

    def y_copy(c, s, peer):
        return pltpu.make_async_remote_copy(
            src_ref=ysend.at[c, s, peer],
            dst_ref=yrecv.at[c, s, chip],
            send_sem=sy_s,
            recv_sem=sy_r.at[c, s],
            device_id=(2 * peer + core, t),
            device_id_type=MESH,
        )

    for c in range(cuts):
        at = c + core * (cuts - 1 - 2 * c)
        columns = pl.ds(pl.multiple_of(at * wide, wide), wide)
        y = sum(
            jnp.dot(xs[b], wq_all[b, :, columns], preferred_element_type=jnp.float32)
            for b in range(2)
        ).reshape(seqs, chips, 2 * steps, wide)
        for s in range(seqs):
            ysend[c, s] = y[s].astype(jnp.bfloat16)
            yown[c, s] = y[s]

            @pl.loop(1, chips)
            def _(k):
                y_copy(c, s, chip_at(chips - k)).start()

    mine = core * nt + t

    def q_copy(c, s, peer_core, peer):
        return pltpu.make_async_remote_copy(
            src_ref=zsend.at[c, s, peer_core],
            dst_ref=qbuf.at[c, s, mine],
            send_sem=sq_s,
            recv_sem=sq_r.at[c, s],
            device_id=(2 * chip + peer_core, peer),
            device_id_type=MESH,
        )

    for c in range(cuts):
        for s in range(seqs):
            whole(yrecv.at[c, s, pl.ds(0, chips - 1)], sy_s, sy_r.at[c, s]).wait_recv()
            z = yown[c, s, chip]
            for k in range(1, chips):
                z = z + yrecv[c, s, chip_at(k)].astype(jnp.float32)
            for i in range(2):
                zsend[c, s, i] = z[i * steps : (i + 1) * steps].astype(zsend.dtype)

            @pl.loop(1, nt)
            def _(k):
                peer = lax.rem(t + nt - k, nt)
                q_copy(c, s, core, peer).start()
                q_copy(c, s, 1 - core, peer).start()

            q_copy(c, s, 1 - core, t).start()
            qbuf[c, s, mine] = zsend[c, s, core]

    drains.append(whole(ysend.at[:, :, pl.ds(0, chips - 1)], sy_s, sy_r.at[0, 0]).wait_send)
    drains.append(whole(qbuf.at[:, :, pl.ds(0, 2 * nt - 1)], sq_s, sq_r.at[0, 0]).wait_send)

    band = group * steps
    owned = heads * steps
    position = t * ctx + lax.broadcasted_iota(jnp.int32, (1, ctx), 1)
    eye = lax.broadcasted_iota(jnp.int32, (owned, HD), 0) == lax.broadcasted_iota(
        jnp.int32, (owned, HD), 1
    )

    def a_copy(peer, s):
        return pltpu.make_async_remote_copy(
            src_ref=asend.at[s, peer],
            dst_ref=arecv.at[s, t],
            send_sem=sa_s,
            recv_sem=sa_r,
            device_id=(d, peer),
            device_id_type=MESH,
        )

    def s_copy(peer, s):
        return pltpu.make_async_remote_copy(
            src_ref=ssend.at[s, peer],
            dst_ref=srecv.at[s, t],
            send_sem=ss_s,
            recv_sem=ss_r,
            device_id=(d, peer),
            device_id_type=MESH,
        )

    def attend(g, s):
        base = pl.multiple_of((g * seqs + s) * band, band)
        q = q_sc[pl.ds(base, band), :].astype(jnp.bfloat16)
        scores = lax.dot_general(
            q, kv[s, g, :, :HD], (((1,), (1,)), ((), ())), preferred_element_type=jnp.float32
        )
        masked = jnp.where(position < lengths[s], scores * scale, NEG)
        best = jnp.max(masked, axis=-1, keepdims=True)
        weights = jnp.exp(masked - best)
        total = jnp.sum(weights, axis=-1, keepdims=True)
        acc = jnp.dot(
            weights.astype(jnp.bfloat16), kv[s, g, :, HD:], preferred_element_type=jnp.float32
        )
        for i in range(per):
            lines = slice(i * owned, (i + 1) * owned)
            asend[s, g * per + i] = acc[lines].astype(asend.dtype)
            for at, stat in enumerate((best, total)):
                ssend[s, g * per + i, at : at + 1, :] = jnp.sum(
                    jnp.where(eye, stat[lines], 0.0), axis=0, keepdims=True
                )

    side = kvh // 2 // cuts
    per = group // heads
    far = (2 * t < nt).astype(jnp.int32)
    pltpu.make_async_copy(cache, kv, sem_kv).wait()
    for c in range(cuts):
        sides = (c, 2 * cuts - 1 - c)
        ready = [i * side + j for i in sides for j in range(side)]
        for s in range(seqs):
            whole(qbuf.at[c, s, pl.ds(0, 2 * nt - 1)], sq_s, sq_r.at[c, s]).wait_recv()
            for i in range(2):
                total = qbuf[c, s, i * nt].astype(jnp.float32)
                for j in range(1, nt):
                    total = total + qbuf[c, s, i * nt + j].astype(jnp.float32)
                for j in range(wide // HD):
                    g = sides[i] * side + j // group
                    r = ((g * seqs + s) * group + j % group) * steps
                    q_sc[r : r + steps, :] = total[:, j * HD : (j + 1) * HD]
            for low, high in zip(ready, ready[::-1]):
                attend(low + (high - low) * far, s)
            for low, high in zip(ready, ready[::-1]):
                for i in range(per):
                    j = (low + (high - low) * far) * per + i

                    @pl.when(t != j)
                    def _():
                        a_copy(j, s).start()
                        s_copy(j, s).start()

    def mine_at(s):
        r = (t * heads // group * seqs + s) * band + lax.rem(t * heads, group) * steps
        return pl.ds(pl.multiple_of(r, owned), owned)

    q_own = jnp.concatenate([q_sc[mine_at(s), :] for s in range(seqs)]).astype(jnp.bfloat16)
    new_keys = fresh[:, :HD].astype(jnp.bfloat16)
    new_values = fresh[:, HD:].astype(jnp.bfloat16)
    new_scores = (
        lax.dot_general(
            q_own, new_keys, (((1,), (1,)), ((), ())), preferred_element_type=jnp.float32
        )
        * scale
    )
    row = lax.broadcasted_iota(jnp.int32, new_scores.shape, 0)
    col = lax.broadcasted_iota(jnp.int32, new_scores.shape, 1)
    col_row = col // kvh
    causal = (
        (lax.rem(col, kvh) == t * heads // group)
        & (row // owned == lax.rem(col_row, seqs))
        & (lax.rem(row, steps) >= col_row // seqs)
    )
    new_masked = jnp.where(causal, new_scores, NEG)
    top = jnp.max(new_masked, axis=-1, keepdims=True)
    new_weights = jnp.where(causal, jnp.exp(new_masked - top), 0.0)
    denom = jnp.sum(new_weights, axis=-1, keepdims=True)
    accum = jnp.dot(
        new_weights.astype(jnp.bfloat16), new_values, preferred_element_type=jnp.float32
    )

    def join(state, best, total, acc):
        top, denom, accum = state
        peak = jnp.maximum(top, best)
        left = jnp.exp(top - peak)
        right = jnp.exp(best - peak)
        return peak, denom * left + total * right, accum * left + acc * right

    def gathered(parts, stats):
        best, total = (
            jnp.concatenate(
                [
                    jnp.sum(jnp.where(eye, x[at : at + 1, :], 0.0), axis=1, keepdims=True)
                    for x in stats
                ]
            )
            for at in range(2)
        )
        return best, total, jnp.concatenate([x.astype(jnp.float32) for x in parts])

    state = join(
        (top, denom, accum),
        *gathered([asend[s, t] for s in range(seqs)], [ssend[s, t] for s in range(seqs)]),
    )
    a_all = whole(arecv.at[:, pl.ds(0, nt - 1)], sa_s, sa_r)
    s_all = whole(srecv.at[:, pl.ds(0, nt - 1)], ss_s, ss_r)
    a_all.wait_recv()
    s_all.wait_recv()

    def a_join(k, state):
        peer = lax.rem(t + k, nt)
        return join(
            state,
            *gathered([arecv[s, peer] for s in range(seqs)], [srecv[s, peer] for s in range(seqs)]),
        )

    top, denom, accum = lax.fori_loop(1, nt, a_join, state)
    r_sc[...] = accum / denom
    for j in range(heads):
        for i in range(steps):
            lines = pl.ds(j * steps + i, seqs, stride=owned)
            out[i, :, j * HD : (j + 1) * HD] = r_sc[lines, :].astype(out.dtype)

    drains.append(a_all.wait_send)
    drains.append(s_all.wait_send)
    for drain in drains:
        drain()


def body(wq_flat, hidden, cache, new_kv, lengths):
    nt = lax.axis_size("tensor")
    n = lax.axis_size("dp")
    t = lax.axis_index("tensor")
    steps, seqs, width = hidden.shape
    rows = steps * seqs
    depth, columns = wq_flat.shape
    kvh, ctx = cache.shape[1], cache.shape[2]
    half = columns // 2
    cuts = 2 if kvh % 4 == 0 else 1
    wide = half // cuts
    heads = QH // nt
    owned = heads * steps
    chips = n // 2
    bf16, f32 = jnp.bfloat16, jnp.float32
    dma = pltpu.SemaphoreType.DMA
    vmem = pl.BlockSpec(memory_space=pltpu.VMEM)
    blocked = depth % 128 != 0
    blocks = hidden
    if blocked:
        blocks = hidden.transpose(1, 0, 2).reshape(rows, n, nt, depth)
        blocks = lax.dynamic_index_in_dim(blocks, t, 2, keepdims=False).astype(f32)
        blocks = blocks.transpose(1, 0, 2)
    tiles = 1 if blocked else depth // HD
    held = (rows, depth) if blocked else (steps, seqs, depth)
    anywhere = pl.BlockSpec(memory_space=pl.ANY)
    result = pl.pallas_call(
        functools.partial(kernel, n, nt, blocked),
        out_shape=pltpu.VMEM((steps, seqs, heads * HD), f32),
        in_specs=[anywhere, anywhere, vmem if blocked else anywhere, anywhere, anywhere, anywhere],
        out_specs=vmem,
        scratch_shapes=[
            pltpu.VMEM(hidden.shape, bf16),
            pltpu.VMEM(new_kv.shape, bf16),
            pltpu.SMEM(lengths.shape, jnp.int32),
            dma((3,)),
            pltpu.VMEM((depth, half), bf16),
            pltpu.VMEM((2, depth, half), bf16),
            pltpu.VMEM(cache.shape, bf16),
            pltpu.VMEM((rows * kvh, 2 * HD), f32),
            pltpu.VMEM((2, tiles, n * rows, depth // tiles), f32),
            pltpu.VMEM((2, n, *held), blocks.dtype),
            pltpu.VMEM((cuts, seqs, chips, 2 * steps, wide), f32),
            pltpu.VMEM((cuts, seqs, chips, 2 * steps, wide), bf16),
            pltpu.VMEM((cuts, seqs, chips, 2 * steps, wide), bf16),
            pltpu.VMEM((cuts, seqs, 2, steps, wide), bf16),
            pltpu.VMEM((cuts, seqs, 2 * nt, steps, wide), bf16),
            pltpu.VMEM((QH * rows, HD), f32),
            pltpu.VMEM((heads * rows, HD), f32),
            pltpu.VMEM((seqs, nt, owned, HD), bf16),
            pltpu.VMEM((seqs, nt, owned, HD), bf16),
            pltpu.VMEM((seqs, nt, 8, HD), f32),
            pltpu.VMEM((seqs, nt, 8, HD), f32),
            dma((2,)),
            dma(()),
            dma(()),
            dma(()),
            dma(()),
            dma((cuts, seqs)),
            dma(()),
            dma(()),
            dma(()),
            dma((cuts, seqs)),
            dma(()),
            dma(()),
            dma(()),
            dma(()),
        ],
        compiler_params=pltpu.CompilerParams(collective_id=0, has_side_effects=True),
    )(lengths, hidden, blocks, new_kv, wq_flat, cache)
    return result.astype(bf16)


def solution(mesh):
    placed = (
        P(("dp", "tensor"), None),
        P(None, "dp", None),
        P("dp", None, "tensor", None),
        P(None, "dp", None, None),
        P("dp"),
    )
    return jax.shard_map(
        body, mesh=mesh, in_specs=placed, out_specs=P(None, "dp", "tensor"), check_vma=False
    )
```

time: 25.9 us -> 24.1 us (0.931)
  Pallas kernels: 25.1 us -> 23.4 us
    pallas_call x1, Pallas kernels: 25.1 us -> 23.4 us  [body(): pl.pallas_call(functools.partial(kernel, n, nt, blocked), out_shape=pltpu...]
where the time goes in v2:
time: 24.1 us; the launch traced here: 24 us
  Pallas kernels  23.4 us (97%)
  other arithmetic  0.62 us (3%)
    pallas_call x1, Pallas kernels, body(): pl.pallas_call(functools.partial(kernel, n, nt, blocked), out_shape=pltpu...  23.4 us
    convert_element_type x1, other arithmetic, body(): return result.astype(bf16)  0.62 us

profile of v2, /device:TPU:0, one launch (start us, length us, event | category | flops | bytes accessed | tf_op | source)
XLA Modules:
  0.0 24.0 jit_solution(10576118545853822481)
XLA Ops:
  0.0 23.4 %shard_map.55 = f32[4,2,1024]{2,1,0:T(2,128)S(1)} custom-call(s32[2]{0:T(128)} %lengths_any.1, bf16[4,2,8192]{2,1,0:T(2,128)(2,1)} %blocks.1, bf16[4,2,8192]{2,1,0:T(2,128)(2,1)} %blocks.1, bf16[4,2,4,256]{3,2,1,0:T(4,128)(2,1)} %new_any.1, bf16[256,4096]{1,0:T(8,128)(2,1)} %wq.1, bf16[2,4,2048,256]{3,2,1,0:T(8,128)(2,1)} %cache.1), custom_call_target="tpu_custom_call" | custom-call | tf_op jit(solution)/shard_map/pallas_call | solution.py:435
  23.4 0.6 %convert_element_type.3 = bf16[4,2,1024]{2,1,0:T(2,128)(2,1)} convert(f32[4,2,1024]{2,1,0:T(2,128)S(1)} %shard_map.55) | non-fusion elementwise | flops 8192 | bytes 49152 | tf_op jit(solution)/shard_map/convert_element_type | solution.py:479

commit v3 on v2

--- a/solution.py
+++ b/solution.py
@@ -162,9 +162,6 @@
     push.start()
     for b in range(2):
         xg[b, d] = columns_of(2 * chip + b)[...]
-    for g in range(kvh):
-        for s in range(seqs):
-            load_kv[s][g].start()
     for i in range(steps):
         for s in range(seqs):
             r = (i * seqs + s) * kvh
@@ -220,7 +217,11 @@
             def _(k):
                 y_copy(c, s, chip_at(chips - k)).start()
 
+    for g in range(kvh):
+        for s in range(seqs):
+            load_kv[s][g].start()
     mine = core * nt + t
+    far = (2 * t < nt).astype(jnp.int32)
 
     def q_copy(c, s, peer_core, peer):
         return pltpu.make_async_remote_copy(
@@ -243,7 +244,7 @@
 
             @pl.loop(1, nt)
             def _(k):
-                peer = lax.rem(t + nt - k, nt)
+                peer = lax.rem(t + nt + k * (1 - 2 * far), nt)
                 q_copy(c, s, core, peer).start()
                 q_copy(c, s, 1 - core, peer).start()
 
@@ -286,9 +287,10 @@
         scores = lax.dot_general(
             q, kv[s, g, :, :HD], (((1,), (1,)), ((), ())), preferred_element_type=jnp.float32
         )
-        masked = jnp.where(position < lengths[s], scores * scale, NEG)
+        masked = jnp.where(position < lengths[s], scores, NEG)
         best = jnp.max(masked, axis=-1, keepdims=True)
-        weights = jnp.exp(masked - best)
+        weights = jnp.exp2((masked - best) * (scale * 1.4426950408889634))
+        best = best * scale
         total = jnp.sum(weights, axis=-1, keepdims=True)
         acc = jnp.dot(
             weights.astype(jnp.bfloat16), kv[s, g, :, HD:], preferred_element_type=jnp.float32
@@ -303,7 +305,6 @@
 
     side = kvh // 2 // cuts
     per = group // heads
-    far = (2 * t < nt).astype(jnp.int32)
     pltpu.make_async_copy(cache, kv, sem_kv).wait()
     for c in range(cuts):
         sides = (c, 2 * cuts - 1 - c)
@@ -320,7 +321,6 @@
                     q_sc[r : r + steps, :] = total[:, j * HD : (j + 1) * HD]
             for low, high in zip(ready, ready[::-1]):
                 attend(low + (high - low) * far, s)
-            for low, high in zip(ready, ready[::-1]):
                 for i in range(per):
                     j = (low + (high - low) * far) * per + i
 

time: 24.1 us -> 23.7 us (0.983)
  Pallas kernels: 23.4 us -> 23 us
    pallas_call x1, Pallas kernels: 23.4 us -> 23 us  [body(): pl.pallas_call(functools.partial(kernel, n, nt, blocked), out_shape=pltpu...]
where the time goes in v3:
time: 23.7 us; the launch traced here: 23.6 us
  Pallas kernels  23 us (97%)
  other arithmetic  0.62 us (3%)
    pallas_call x1, Pallas kernels, body(): pl.pallas_call(functools.partial(kernel, n, nt, blocked), out_shape=pltpu...  23 us
    convert_element_type x1, other arithmetic, body(): return result.astype(bf16)  0.62 us

profile of v3, /device:TPU:0, one launch (start us, length us, event | category | flops | bytes accessed | tf_op | source)
XLA Modules:
  0.0 23.6 jit_solution(4480556802360241126)
XLA Ops:
  0.0 23.0 %shard_map.55 = f32[4,2,1024]{2,1,0:T(2,128)S(1)} custom-call(s32[2]{0:T(128)} %lengths_any.1, bf16[4,2,8192]{2,1,0:T(2,128)(2,1)} %blocks.1, bf16[4,2,8192]{2,1,0:T(2,128)(2,1)} %blocks.1, bf16[4,2,4,256]{3,2,1,0:T(4,128)(2,1)} %new_any.1, bf16[256,4096]{1,0:T(8,128)(2,1)} %wq.1, bf16[2,4,2048,256]{3,2,1,0:T(8,128)(2,1)} %cache.1), custom_call_target="tpu_custom_call" | custom-call | tf_op jit(solution)/shard_map/pallas_call | solution.py:435
  23.0 0.6 %convert_element_type.3 = bf16[4,2,1024]{2,1,0:T(2,128)(2,1)} convert(f32[4,2,1024]{2,1,0:T(2,128)S(1)} %shard_map.55) | non-fusion elementwise | flops 8192 | bytes 49152 | tf_op jit(solution)/shard_map/convert_element_type | solution.py:479

commit v4 on v3

--- a/solution.py
+++ b/solution.py
@@ -213,8 +213,7 @@
             ysend[c, s] = y[s].astype(jnp.bfloat16)
             yown[c, s] = y[s]
 
-            @pl.loop(1, chips)
-            def _(k):
+            for k in range(1, chips):
                 y_copy(c, s, chip_at(chips - k)).start()
 
     for g in range(kvh):
@@ -242,8 +241,7 @@
             for i in range(2):
                 zsend[c, s, i] = z[i * steps : (i + 1) * steps].astype(zsend.dtype)
 
-            @pl.loop(1, nt)
-            def _(k):
+            for k in range(1, nt):
                 peer = lax.rem(t + nt + k * (1 - 2 * far), nt)
                 q_copy(c, s, core, peer).start()
                 q_copy(c, s, 1 - core, peer).start()
@@ -393,7 +391,9 @@
             *gathered([arecv[s, peer] for s in range(seqs)], [srecv[s, peer] for s in range(seqs)]),
         )
 
-    top, denom, accum = lax.fori_loop(1, nt, a_join, state)
+    for k in range(1, nt):
+        state = a_join(k, state)
+    top, denom, accum = state
     r_sc[...] = accum / denom
     for j in range(heads):
         for i in range(steps):

time: 23.7 us -> 23.4 us (0.987)
  Pallas kernels: 23 us -> 22.6 us
    pallas_call x1, Pallas kernels: 23 us -> 22.6 us  [body(): pl.pallas_call(functools.partial(kernel, n, nt, blocked), out_shape=pltpu...]
where the time goes in v4:
time: 23.4 us; the launch traced here: 23.3 us
  Pallas kernels  22.6 us (97%)
  other arithmetic  0.62 us (3%)
    pallas_call x1, Pallas kernels, body(): pl.pallas_call(functools.partial(kernel, n, nt, blocked), out_shape=pltpu...  22.6 us
    convert_element_type x1, other arithmetic, body(): return result.astype(bf16)  0.62 us

profile of v4, /device:TPU:0, one launch (start us, length us, event | category | flops | bytes accessed | tf_op | source)
XLA Modules:
  0.0 23.3 jit_solution(6100561133892079667)
XLA Ops:
  0.0 22.6 %shard_map.55 = f32[4,2,1024]{2,1,0:T(2,128)S(1)} custom-call(s32[2]{0:T(128)} %lengths_any.1, bf16[4,2,8192]{2,1,0:T(2,128)(2,1)} %blocks.1, bf16[4,2,8192]{2,1,0:T(2,128)(2,1)} %blocks.1, bf16[4,2,4,256]{3,2,1,0:T(4,128)(2,1)} %new_any.1, bf16[256,4096]{1,0:T(8,128)(2,1)} %wq.1, bf16[2,4,2048,256]{3,2,1,0:T(8,128)(2,1)} %cache.1), custom_call_target="tpu_custom_call" | custom-call | tf_op jit(solution)/shard_map/pallas_call | solution.py:435
  22.6 0.6 %convert_element_type.3 = bf16[4,2,1024]{2,1,0:T(2,128)(2,1)} convert(f32[4,2,1024]{2,1,0:T(2,128)S(1)} %shard_map.55) | non-fusion elementwise | flops 8192 | bytes 49152 | tf_op jit(solution)/shard_map/convert_element_type | solution.py:479
